TPU v7x, 32 devices: a whole 2x2x4 slice. The times are simulated.
32 devices in a mesh: batch: 16 (over z, y, core), tensor: 2 (over x).
Axes of the slice: x: 2, y: 2, z: 4, core: 2. Of those that a mesh axis runs over, the one named last changes fastest.
Arguments:
- block_in: bfloat16 [2, 16384, 1024], P(None, ('batch', 'tensor')), may hold values from -6 to 6
- lengths: int32 [2, 16, 4], P(None, 'batch'), may hold values from 1 to 512, 1024 in all within a row
- norm_gains: float32 [3, 1024], replicated, may hold values from 0.5 to 1.5
- qkv_weight: bfloat16 [3, 1024, 1024], P(None, 'batch', 'tensor'), may hold values from -0.1875 to 0.1875
- head_scale: float32 [16], P('tensor'), may hold values from 0.5 to 2
- out_weight: bfloat16 [1024, 1024], P('tensor', 'batch'), may hold values from -0.1875 to 0.1875
- up_weight: bfloat16 [1024, 4096], P('batch', 'tensor'), may hold values from -0.7875 to 0.7875
- mid_gain: float32 [4096], P('tensor'), may hold values from 0.5 to 1.5
- down_weight: bfloat16 [4096, 1024], P('tensor', 'batch'), may hold values from -0.39375 to 0.39375
- cotangent: bfloat16 [2, 16384, 1024], P(None, ('batch', 'tensor')), may hold values from -6 to 6
Outputs:
- block_out: bfloat16 [2, 16384, 1024], P(None, ('batch', 'tensor'))
- grad_in: bfloat16 [2, 16384, 1024], P(None, ('batch', 'tensor'))
- grad_gains: float32 [3, 1024], replicated
- grad_qkv: float32 [3, 1024, 1024], P(None, 'batch', 'tensor')
- grad_scale: float32 [16], P('tensor')
- grad_proj: float32 [1024, 1024], P('tensor', 'batch')
- grad_up: float32 [1024, 4096], P('batch', 'tensor')
- grad_mid: float32 [4096], P('tensor')
- grad_down: float32 [4096, 1024], P('tensor', 'batch')
Inputs may be any that keep to these rules, and one draw needn't show every extreme that they name: lengths[m, b] holds the lengths of the 4 sequences packed in order into the 1024 rows of group b in micro-batch m; they sum to 1024.
All inputs are finite; a program needn't handle non-finite values.
Results may differ from a plain program's by a relative error of at most 0.019.
Values may be sent and summed in bfloat16 or wider, within the bound.
No kernel may reach another device: no remote copies, remote signals or barrier semaphores. Data moves between devices by JAX's collectives and lax.ppermute only.
A program may use at most 256 MiB of HBM per device.

v0:
```python
import jax
import jax.numpy as jnp
from jax import lax
from jax.sharding import PartitionSpec as P

eps = 1e-05


def normalize(values):
    centred = values - jnp.mean(values, axis=-1, keepdims=True)
    factor = lax.rsqrt(jnp.mean(centred * centred, axis=-1, keepdims=True) + eps)
    return (centred * factor, factor)


def norm_back(unit, factor, grad):
    return factor * (
        grad
        - jnp.mean(grad, axis=-1, keepdims=True)
        - unit * jnp.mean(grad * unit, axis=-1, keepdims=True)
    )


def segment_ids(seq_lengths, group_rows):
    places = jnp.arange(group_rows, dtype=jnp.int32)
    ends = jnp.cumsum(seq_lengths)
    seg_ids = jnp.sum((places[:, None] >= ends[None, :]).astype(jnp.int32), axis=1)
    return (seg_ids, places)


def visible_block(seg_ids, places, first_row, block_rows):
    seg_block = lax.dynamic_slice_in_dim(seg_ids, first_row, block_rows, 0)
    place_block = lax.dynamic_slice_in_dim(places, first_row, block_rows, 0)
    return (seg_block[:, None] == seg_ids[None, :]) & (place_block[:, None] >= places[None, :])


def attend_forward(queries, all_keys, values, seg_ids, places, block_rows, factor):
    group_rows = queries.shape[0]

    def one_block(first_row):
        query_block = lax.dynamic_slice_in_dim(queries, first_row, block_rows, 0)
        visible = visible_block(seg_ids, places, first_row, block_rows)
        scores = (
            jnp.einsum("qhd,khd->hqk", query_block, all_keys, preferred_element_type=jnp.float32)
            * factor
        )
        scores = jnp.where(visible[None], scores, -1e30)
        row_max = jnp.max(scores, axis=-1, keepdims=True)
        shifted = jnp.exp(scores - row_max)
        row_sum = jnp.sum(shifted, axis=-1, keepdims=True)
        weights_low = (shifted / row_sum).astype(jnp.bfloat16)
        attended = jnp.einsum(
            "hqk,khd->qhd", weights_low, values, preferred_element_type=jnp.float32
        )
        return (attended, (row_max + jnp.log(row_sum))[..., 0])

    firsts = jnp.arange(group_rows // block_rows, dtype=jnp.int32) * block_rows
    attended, log_sums = lax.map(one_block, firsts)
    return (attended.reshape(queries.shape), log_sums)


def attend_backward(
    queries, all_keys, values, seg_ids, places, block_rows, factor, log_sums, out_grad
):
    group_rows = queries.shape[0]

    def one_block(totals, pieces):
        key_grad, value_grad = totals
        first_row, log_block = pieces
        query_block = lax.dynamic_slice_in_dim(queries, first_row, block_rows, 0)
        grad_block = lax.dynamic_slice_in_dim(out_grad, first_row, block_rows, 0)
        visible = visible_block(seg_ids, places, first_row, block_rows)
        scores = (
            jnp.einsum("qhd,khd->hqk", query_block, all_keys, preferred_element_type=jnp.float32)
            * factor
        )
        scores = jnp.where(visible[None], scores, -1e30)
        probs = jnp.exp(scores - log_block[..., None])
        value_grad = value_grad + jnp.einsum(
            "hqk,qhd->khd",
            probs.astype(jnp.bfloat16),
            grad_block,
            preferred_element_type=jnp.float32,
        )
        prob_grad = jnp.einsum(
            "qhd,khd->hqk", grad_block, values, preferred_element_type=jnp.float32
        )
        inner = jnp.sum(probs * prob_grad, axis=-1, keepdims=True)
        score_grad = (probs * (prob_grad - inner)).astype(jnp.bfloat16)
        query_grad = (
            jnp.einsum("hqk,khd->qhd", score_grad, all_keys, preferred_element_type=jnp.float32)
            * factor
        )
        key_grad = (
            key_grad
            + jnp.einsum(
                "hqk,qhd->khd", score_grad, query_block, preferred_element_type=jnp.float32
            )
            * factor
        )
        return ((key_grad, value_grad), query_grad)

    zero_grad = jnp.zeros(queries.shape, jnp.float32)
    firsts = jnp.arange(group_rows // block_rows, dtype=jnp.int32) * block_rows
    (key_grad, value_grad), query_grad = lax.scan(
        one_block, (zero_grad, zero_grad), (firsts, log_sums)
    )
    return (query_grad.reshape(queries.shape), key_grad, value_grad)


def body(
    block_in,
    lengths,
    norm_gains,
    qkv_weight,
    head_scale,
    out_weight,
    up_weight,
    mid_gain,
    down_weight,
    cotangent,
):
    tensor_count = lax.axis_size("tensor")
    tensor_rank = lax.axis_index("tensor")
    qkv_full, out_full, up_full, down_full = (
        lax.all_gather(qkv_weight, "batch", axis=1, tiled=True),
        lax.all_gather(out_weight, "batch", axis=1, tiled=True),
        lax.all_gather(up_weight, "batch", axis=0, tiled=True),
        lax.all_gather(down_weight, "batch", axis=1, tiled=True),
    )
    micro_count, own_rows, model_width = block_in.shape
    group_rows = own_rows * tensor_count
    local_heads = head_scale.shape[0]
    head_size = qkv_full.shape[2] // local_heads
    local_hidden = mid_gain.shape[0]
    hidden_total = local_hidden * tensor_count
    block_rows = min(512, group_rows)
    factor = head_size ** (-0.5)
    heads_shape = (group_rows, local_heads, head_size)
    row_start = tensor_rank * own_rows
    qkv_acc = jnp.zeros(qkv_full.shape, jnp.float32)
    proj_acc = jnp.zeros(out_full.shape, jnp.float32)
    up_acc = jnp.zeros(up_full.shape, jnp.float32)
    down_acc = jnp.zeros(down_full.shape, jnp.float32)
    first_gain = jnp.zeros((model_width,), jnp.float32)
    second_gain = jnp.zeros((model_width,), jnp.float32)
    third_gain = jnp.zeros((model_width,), jnp.float32)
    mid_acc = jnp.zeros((local_hidden,), jnp.float32)
    scale_acc = jnp.zeros((local_heads,), jnp.float32)
    outputs = []
    input_grads = []
    for micro_step in range(micro_count):
        seg_ids, places = segment_ids(lengths[micro_step, 0], group_rows)
        x_rows = block_in[micro_step].astype(jnp.float32)
        input_unit, input_factor = normalize(x_rows)
        first_own = (input_unit * norm_gains[0]).astype(jnp.bfloat16)
        first_all = lax.all_gather(first_own, "tensor", axis=0, tiled=True)
        projected = jnp.einsum(
            "gd,cde->cge", first_all, qkv_full, preferred_element_type=jnp.float32
        ).astype(jnp.bfloat16)
        queries = projected[0].reshape(heads_shape)
        all_keys = projected[1].reshape(heads_shape)
        values = projected[2].reshape(heads_shape)
        attended, log_sums = attend_forward(
            queries, all_keys, values, seg_ids, places, block_rows, factor
        )
        scaled = (attended * head_scale[None, :, None]).astype(jnp.bfloat16).reshape(group_rows, -1)
        whole_mixed = lax.psum(
            jnp.dot(scaled, out_full, preferred_element_type=jnp.float32), "tensor"
        )
        mixed_own = lax.dynamic_slice_in_dim(whole_mixed, row_start, own_rows, 0)
        mixed_unit, mixed_factor = normalize(mixed_own)
        resid = x_rows + mixed_unit * norm_gains[1]
        resid_unit, resid_factor = normalize(resid)
        third_own = (resid_unit * norm_gains[2]).astype(jnp.bfloat16)
        third_all = lax.all_gather(third_own, "tensor", axis=0, tiled=True)
        hidden = jnp.dot(third_all, up_full, preferred_element_type=jnp.float32)
        activated = jax.nn.gelu(hidden)
        act_sum, act_squares = lax.psum(
            (jnp.sum(activated, axis=1), jnp.sum(activated * activated, axis=1)), "tensor"
        )
        act_mean = act_sum / hidden_total
        act_factor = lax.rsqrt(act_squares / hidden_total - act_mean * act_mean + eps)[:, None]
        act_unit = (activated - act_mean[:, None]) * act_factor
        narrow = (act_unit * mid_gain).astype(jnp.bfloat16)
        feed_own = lax.psum_scatter(
            jnp.dot(narrow, down_full, preferred_element_type=jnp.float32).astype(jnp.bfloat16),
            "tensor",
            scatter_dimension=0,
            tiled=True,
        ).astype(jnp.float32)
        outputs.append((resid + feed_own).astype(jnp.bfloat16))
        out_rows = cotangent[micro_step].astype(jnp.float32)
        feed_grad = lax.all_gather(out_rows.astype(jnp.bfloat16), "tensor", axis=0, tiled=True)
        down_acc = down_acc + jnp.einsum(
            "gf,gd->fd", narrow, feed_grad, preferred_element_type=jnp.float32
        )
        narrow_grad = jnp.einsum(
            "gd,fd->gf", feed_grad, down_full, preferred_element_type=jnp.float32
        )
        mid_acc = mid_acc + jnp.sum(narrow_grad * act_unit, axis=0)
        gained = narrow_grad * mid_gain
        back_sum, back_inner = lax.psum(
            (jnp.sum(gained, axis=1), jnp.sum(gained * act_unit, axis=1)), "tensor"
        )
        act_grad = act_factor * (
            gained
            - back_sum[:, None] / hidden_total
            - act_unit * back_inner[:, None] / hidden_total
        )
        gelu_pull = jax.vjp(jax.nn.gelu, hidden)[1]
        hidden_grad = gelu_pull(act_grad)[0].astype(jnp.bfloat16)
        up_acc = up_acc + jnp.einsum(
            "gd,gf->df", third_all, hidden_grad, preferred_element_type=jnp.float32
        )
        third_grad = lax.psum_scatter(
            jnp.einsum("gf,df->gd", hidden_grad, up_full, preferred_element_type=jnp.float32),
            "tensor",
            scatter_dimension=0,
            tiled=True,
        )
        third_gain = third_gain + jnp.sum(third_grad * resid_unit, axis=0)
        resid_grad = out_rows + norm_back(resid_unit, resid_factor, third_grad * norm_gains[2])
        second_gain = second_gain + jnp.sum(resid_grad * mixed_unit, axis=0)
        mixed_grad = norm_back(mixed_unit, mixed_factor, resid_grad * norm_gains[1]).astype(
            jnp.bfloat16
        )
        mixed_all = lax.all_gather(mixed_grad, "tensor", axis=0, tiled=True)
        proj_acc = proj_acc + jnp.einsum(
            "ge,gd->ed", scaled, mixed_all, preferred_element_type=jnp.float32
        )
        scaled_grad = jnp.einsum(
            "gd,ed->ge", mixed_all, out_full, preferred_element_type=jnp.float32
        ).reshape(heads_shape)
        scale_acc = scale_acc + jnp.sum(scaled_grad * attended, axis=(0, 2))
        attended_grad = (scaled_grad * head_scale[None, :, None]).astype(jnp.bfloat16)
        query_grad, key_grad, value_grad = attend_backward(
            queries, all_keys, values, seg_ids, places, block_rows, factor, log_sums, attended_grad
        )
        proj_grads = jnp.stack(
            [
                query_grad.reshape(group_rows, -1),
                key_grad.reshape(group_rows, -1),
                value_grad.reshape(group_rows, -1),
            ]
        ).astype(jnp.bfloat16)
        qkv_acc = qkv_acc + jnp.einsum(
            "gd,cge->cde", first_all, proj_grads, preferred_element_type=jnp.float32
        )
        first_grad = lax.psum_scatter(
            jnp.einsum(
                "cge,cde->gd", proj_grads, qkv_full, preferred_element_type=jnp.float32
            ).astype(jnp.bfloat16),
            "tensor",
            scatter_dimension=0,
            tiled=True,
        ).astype(jnp.float32)
        first_gain = first_gain + jnp.sum(first_grad * input_unit, axis=0)
        input_grads.append(
            (resid_grad + norm_back(input_unit, input_factor, first_grad * norm_gains[0])).astype(
                jnp.bfloat16
            )
        )
    qkv_grad, proj_grad, up_grad, down_grad = (
        lax.psum_scatter(
            qkv_acc.astype(jnp.bfloat16), "batch", scatter_dimension=1, tiled=True
        ).astype(jnp.float32),
        lax.psum_scatter(
            proj_acc.astype(jnp.bfloat16), "batch", scatter_dimension=1, tiled=True
        ).astype(jnp.float32),
        lax.psum_scatter(
            up_acc.astype(jnp.bfloat16), "batch", scatter_dimension=0, tiled=True
        ).astype(jnp.float32),
        lax.psum_scatter(
            down_acc.astype(jnp.bfloat16), "batch", scatter_dimension=1, tiled=True
        ).astype(jnp.float32),
    )
    mid_full = lax.dynamic_update_slice_in_dim(
        jnp.zeros((hidden_total,), jnp.float32), mid_acc, tensor_rank * local_hidden, 0
    )
    scale_full = lax.dynamic_update_slice_in_dim(
        jnp.zeros((local_heads * tensor_count,), jnp.float32),
        scale_acc,
        tensor_rank * local_heads,
        0,
    )
    gains_sum, mid_sum, scale_sum = lax.psum(
        (jnp.stack([first_gain, second_gain, third_gain]), mid_full, scale_full),
        ("batch", "tensor"),
    )
    mid_own = lax.dynamic_slice_in_dim(mid_sum, tensor_rank * local_hidden, local_hidden, 0)
    scale_own = lax.dynamic_slice_in_dim(scale_sum, tensor_rank * local_heads, local_heads, 0)
    return (
        jnp.stack(outputs),
        jnp.stack(input_grads),
        gains_sum,
        qkv_grad,
        scale_own,
        proj_grad,
        up_grad,
        mid_own,
        down_grad,
    )


def solution(mesh):
    in_specs = (
        P(None, ("batch", "tensor"), None),
        P(None, "batch", None),
        P(),
        P(None, "batch", "tensor"),
        P("tensor"),
        P("tensor", "batch"),
        P("batch", "tensor"),
        P("tensor"),
        P("tensor", "batch"),
        P(None, ("batch", "tensor"), None),
    )
    out_specs = (
        P(None, ("batch", "tensor"), None),
        P(None, ("batch", "tensor"), None),
        P(),
        P(None, "batch", "tensor"),
        P("tensor"),
        P("tensor", "batch"),
        P("batch", "tensor"),
        P("tensor"),
        P("tensor", "batch"),
    )
    return jax.shard_map(body, mesh=mesh, in_specs=in_specs, out_specs=out_specs, check_vma=False)
```

profile of v0, /device:TPU:0, one launch (start us, length us, event | category | flops | bytes accessed | tf_op | source)
XLA Modules:
  0.0 1623.8 jit_solution(3066448921522963415)
XLA Ops:
  16.8 32.0 %all-gather.15.cloned.1.call-done = bf16[1024,1024]{1,0:T(8,128)(2,1)} async-done(((bf16[512,1024]{1,0:T(8,128)(2,1)}), bf16[1024,1024]{1,0:T(8,128)(2,1)}) %all-gather.15.cloned.1.call-update) | async-done | bytes 2097168 | tf_op jit(solution)/shard_map/all_gather | solution.py:156
  48.8 47.4 %all-gather.17.cloned.1.call-done = bf16[3,1024,512]{2,1,0:T(8,128)(2,1)} async-done(((bf16[3,64,512]{2,1,0:T(8,128)(2,1)}), bf16[3,1024,512]{2,1,0:T(8,128)(2,1)}) %all-gather.17.cloned.1.call-update) | async-done | bytes 3145744 | tf_op jit(solution)/shard_map/all_gather | solution.py:125
  105.5 75.3 %while.58 = (s32[]{:T(128)}, f32[2,512,8,64]{1,0,3,2:T(2,128)}, f32[2,8,512]{2,1,0:T(8,128)S(1)}, s32[2]{0:T(128)S(1)}, s32[1024]{0:T(1024)S(1)}, /*index=5*/s32...) while((s32[]{:T(128)}, f32[2,512,8,64]{1,0,3,2:T(2,128)}, ...), condition=%wide.region_7.8_spmd.clone, body=%wide.region_4.7_spmd.clone.sunk | while | flops 1125642240 | bytes 60444856 | solution.py:57
  123.5 19.6 %dynamic_update_slice.49 = f32[2,512,8,64]{1,0,3,2:T(2,128)} dynamic-update-slice(f32[2,512,8,64]{1,0,3,2:T(2,128)} %get-tuple-element.984, f32[1,512,8,64]{1,0,3,2:T(1,128)S(1)} %copy.129, s32[]{:T(128)} %get-tuple-element.983, s32[]{:T(128)} %constant.141.clone.1..sunk, s32[]{:T(128)} %constant.141.clone.1..sunk, s32[]{:T(128)} %constant.141.clone.1..sunk) | dynamic-update-slice | bytes 2097156 | tf_op jit(solution)/shard_map/while/body/jit(dynamic_update_index_in_dim)/dynamic_update_slice | solution.py:57
  160.8 19.6 %dynamic_update_slice.49 = f32[2,512,8,64]{1,0,3,2:T(2,128)} dynamic-update-slice(f32[2,512,8,64]{1,0,3,2:T(2,128)} %get-tuple-element.984, f32[1,512,8,64]{1,0,3,2:T(1,128)S(1)} %copy.129, s32[]{:T(128)} %get-tuple-element.983, s32[]{:T(128)} %constant.141.clone.1..sunk, s32[]{:T(128)} %constant.141.clone.1..sunk, s32[]{:T(128)} %constant.141.clone.1..sunk) | dynamic-update-slice | bytes 2097156 | tf_op jit(solution)/shard_map/while/body/jit(dynamic_update_index_in_dim)/dynamic_update_slice | solution.py:57
  191.5 74.9 %while.59 = (s32[]{:T(128)}, f32[2,512,8,64]{1,0,3,2:T(2,128)}, f32[2,8,512]{2,1,0:T(8,128)S(1)}, s32[2]{0:T(128)S(1)}, s32[1024]{0:T(1024)S(1)}, /*index=5*/s32...) while((s32[]{:T(128)}, f32[2,512,8,64]{1,0,3,2:T(2,128)}, ...), condition=%wide.region_25.26_spmd.clone, body=%wide.region_22.25_spmd.clone.sunk | while | flops 1125642240 | bytes 60444856 | solution.py:57
  209.3 19.6 %dynamic_update_slice.51 = f32[2,512,8,64]{1,0,3,2:T(2,128)} dynamic-update-slice(f32[2,512,8,64]{1,0,3,2:T(2,128)} %get-tuple-element.948, f32[1,512,8,64]{1,0,3,2:T(1,128)S(1)} %copy.130, s32[]{:T(128)} %get-tuple-element.947, s32[]{:T(128)} %constant.141.clone.1..sunk.1, s32[]{:T(128)} %constant.141.clone.1..sunk.1, s32[]{:T(128)} %constant.141.clone.1..sunk.1) | dynamic-update-slice | bytes 2097156 | tf_op jit(solution)/shard_map/while/body/jit(dynamic_update_index_in_dim)/dynamic_update_slice | solution.py:57
  246.6 19.6 %dynamic_update_slice.51 = f32[2,512,8,64]{1,0,3,2:T(2,128)} dynamic-update-slice(f32[2,512,8,64]{1,0,3,2:T(2,128)} %get-tuple-element.948, f32[1,512,8,64]{1,0,3,2:T(1,128)S(1)} %copy.130, s32[]{:T(128)} %get-tuple-element.947, s32[]{:T(128)} %constant.141.clone.1..sunk.1, s32[]{:T(128)} %constant.141.clone.1..sunk.1, s32[]{:T(128)} %constant.141.clone.1..sunk.1) | dynamic-update-slice | bytes 2097156 | tf_op jit(solution)/shard_map/while/body/jit(dynamic_update_index_in_dim)/dynamic_update_slice | solution.py:57
  286.0 192.8 %all-reduce.10.cloned.1.call-done = (f32[1024,1024]{1,0:T(8,128)}, f32[1024,1024]{1,0:T(8,128)}) async-done(((f32[1024,1024]{1,0:T(8,128)}, f32[1024,1024]{1,0:T(8,128)}), (f32[1024,1024]{1,0:T(8,128)}, f32[1024,1024]{1,0:T(8,128)})) %all-reduce.10.cloned.1.call-update) | async-done | bytes 8388624 | tf_op jit(solution)/shard_map/psum | solution.py:167
  491.7 22.0 %all-gather.37.cloned.1.call-done = bf16[1,1024,1024]{2,1,0:T(8,128)(2,1)} async-done(((bf16[1,512,1024]{2,1,0:T(8,128)(2,1)}), bf16[1,1024,1024]{2,1,0:T(8,128)(2,1)}) %all-gather.37.cloned.1.call-update) | async-done | bytes 2097168 | tf_op jit(solution)/shard_map/all_gather | solution.py:193
  513.7 52.8 %all-gather.25.cloned.1.call-done = bf16[2048,1024]{0,1:T(8,128)(2,1)} async-done(((bf16[2048,64]{0,1:T(8,128)(2,1)}), bf16[2048,1024]{0,1:T(8,128)(2,1)}) %all-gather.25.cloned.1.call-update) | async-done | bytes 4194320 | tf_op jit(solution)/shard_map/all_gather | solution.py:128
  566.5 10.5 fusion.98
  577.0 40.7 %all-gather.23.cloned.1.call-done = bf16[1024,2048]{1,0:T(8,128)(2,1)} async-done(((bf16[64,2048]{1,0:T(8,128)(2,1)}), bf16[1024,2048]{1,0:T(8,128)(2,1)}) %all-gather.23.cloned.1.call-update) | async-done | bytes 4194320 | tf_op jit(solution)/shard_map/all_gather | solution.py:127
  617.7 33.8 %all-gather.21.cloned.1.call-done = bf16[1024,1024]{1,0:T(8,128)(2,1)} async-done(((bf16[512,1024]{1,0:T(8,128)(2,1)}), bf16[1024,1024]{1,0:T(8,128)(2,1)}) %all-gather.21.cloned.1.call-update) | async-done | bytes 2097168 | tf_op jit(solution)/shard_map/all_gather | solution.py:175
  651.5 10.2 fusion.120
  661.7 24.3 %all-gather.29.cloned.1.call-done = bf16[1024,1024]{1,0:T(8,128)(2,1)} async-done(((bf16[512,1024]{1,0:T(8,128)(2,1)}), bf16[1024,1024]{1,0:T(8,128)(2,1)}) %all-gather.29.cloned.1.call-update) | async-done | bytes 2097168 | tf_op jit(solution)/shard_map/all_gather | solution.py:175
  686.0 10.0 fusion.121
  696.0 7.2 all-reduce.3
  703.3 17.8 %all-gather.35.cloned.1.call-done = bf16[1,1024,1024]{2,1,0:T(8,128)(2,1)} async-done(((bf16[1,512,1024]{2,1,0:T(8,128)(2,1)}), bf16[1,1024,1024]{2,1,0:T(8,128)(2,1)}) %all-gather.35.cloned.1.call-update) | async-done | bytes 2097168 | tf_op jit(solution)/shard_map/all_gather | solution.py:193
  721.1 20.2 %multiply_reduce_fusion.3 = (f32[2048]{0:T(1024)}, f32[1024]{0:T(1024)S(1)}, f32[1024]{0:T(1024)S(1)}, f32[1024]{0:T(1024)S(1)}, f32[1024]{0:T(1024)S(1)}, /*index=5*/f32[2048]{0:T(1024)}, f32[1024,2048]{1,0:T(8,128)}) fusion(f32[1024]{0:T(1024)S(1)} %get-tuple-element.645, f32[1024]{0:T(1024)S(1)} %get-tuple-element.644, ...), kind=kOutput, calls=%fused_computation.90 | convolution fusion | flops 4362067968 | bytes 39903232 | tf_op jit(solution)/shard_map/gd,fd->gf/dot_general | solution.py:197
  741.3 6.9 all-reduce.2
  748.2 22.7 %fusion.54 = (bf16[1024,2048]{1,0:T(8,128)(2,1)S(1)}, bf16[1024,2048]{1,0:T(8,128)(2,1)}, bf16[1024,2048]{1,0:T(8,128)(2,1)}) fusion(f32[1024,2048]{1,0:T(8,128)} %get-tuple-element.655, f32[1024,2048]{1,0:T(8,128)} %get-tuple-element.656, f32[1024]{0:T(1024)S(1)} %get-tuple-element.592, f32[1024]{0:T(1024)S(1)} %broadcast_multiply_fusion.1, ...), kind=kLoop, calls=%fused_computation.80 | loop fusion | flops 125829120 | bytes 46178304 | tf_op jit(solution)/shard_map/convert_element_type | solution.py:211
  779.0 9.3 convolution_convert_fusion.1
  788.4 9.9 fusion.131
  798.4 11.1 convolution_convert_fusion
  809.6 25.0 %reduce-scatter.14.cloned.1.call-done = f32[512,1024]{1,0:T(8,128)} async-done(((f32[1024,1024]{1,0:T(8,128)}), f32[512,1024]{1,0:T(8,128)}) %reduce-scatter.14.cloned.1.call-update) | async-done | bytes 2097168 | tf_op jit(solution)/shard_map/reduce_scatter | solution.py:215
  837.6 31.8 %reduce-scatter.10.cloned.1.call-done = bf16[512,1024]{1,0:T(8,128)(2,1)} async-done(((bf16[1024,1024]{1,0:T(8,128)(2,1)}), bf16[512,1024]{1,0:T(8,128)(2,1)}) %reduce-scatter.10.cloned.1.call-update) | async-done | bytes 1048592 | tf_op jit(solution)/shard_map/reduce_scatter | solution.py:185
  869.3 56.5 %reduce-scatter.18.cloned.1.call-done = f32[512,1024]{1,0:T(8,128)} async-done(((f32[1024,1024]{1,0:T(8,128)}), f32[512,1024]{1,0:T(8,128)}) %reduce-scatter.18.cloned.1.call-update) | async-done | bytes 2097168 | tf_op jit(solution)/shard_map/reduce_scatter | solution.py:215
  925.8 7.2 multiply_reduce_fusion.15
  933.1 26.8 %reduce-scatter.12.cloned.1.call-done = bf16[512,1024]{1,0:T(8,128)(2,1)} async-done(((bf16[1024,1024]{1,0:T(8,128)(2,1)}), bf16[512,1024]{1,0:T(8,128)(2,1)}) %reduce-scatter.12.cloned.1.call-update) | async-done | bytes 1048592 | tf_op jit(solution)/shard_map/reduce_scatter | solution.py:185
  969.2 7.6 fusion.100
  976.8 10.9 add_convert_fusion
  989.2 6.5 fusion.132
  1008.6 27.7 %all-gather.31.cloned.1.call-done = bf16[1024,1024]{1,0:T(8,128)(2,1)} async-done(((bf16[512,1024]{1,0:T(8,128)(2,1)}), bf16[1024,1024]{1,0:T(8,128)(2,1)}) %all-gather.31.cloned.1.call-update) | async-done | bytes 2097168 | tf_op jit(solution)/shard_map/all_gather | solution.py:227
  1043.9 123.0 %while.60 = (s32[]{:T(128)}, f32[1024,8,64]{0,2,1:T(8,128)}, f32[1024,8,64]{0,2,1:T(8,128)}, bf16[2,512,8,64]{1,3,2,0:T(8,128)(2,1)}, s32[2]{0:T(128)S(1)}, /*in...) while((s32[]{:T(128)}, f32[1024,8,64]{0,2,1:T(8,128)}, ...), condition=%wide.region_47.48_spmd.clone.clone, body=%wide.region_45.47_spmd.clone.clone.sunk | while | flops 2726555648 | bytes 208769808 | solution.py:104
  1047.5 10.5 fusion.228
  1058.0 13.9 multiply_reduce_fusion.30
  1071.9 14.9 multiply_convert_fusion.20
  1086.9 6.7 bitcast_add_fusion.8
  1093.6 7.6 fusion.229
  1108.5 9.6 fusion.228
  1118.1 13.7 multiply_reduce_fusion.30
  1131.8 15.4 multiply_convert_fusion.20
  1147.2 7.2 bitcast_add_fusion.8
  1154.5 7.6 fusion.229
  1168.0 119.8 %while.61 = (s32[]{:T(128)}, f32[1024,8,64]{0,2,1:T(8,128)}, f32[1024,8,64]{0,2,1:T(8,128)}, bf16[2,512,8,64]{1,3,2,0:T(8,128)(2,1)}, s32[2]{0:T(128)S(1)}, /*in...) while((s32[]{:T(128)}, f32[1024,8,64]{0,2,1:T(8,128)}, ...), condition=%wide.region_62.63_spmd.clone.clone, body=%wide.region_60.62_spmd.clone.clone.sunk | while | flops 2726555648 | bytes 212964144 | solution.py:104
  1171.4 9.6 fusion.239
  1181.0 13.7 multiply_reduce_fusion.31
  1194.7 14.8 multiply_convert_fusion.21
  1209.5 6.7 bitcast_add_fusion.10
  1216.2 7.7 fusion.240
  1230.1 9.6 fusion.239
  1239.7 13.6 multiply_reduce_fusion.31
  1253.3 14.8 multiply_convert_fusion.21
  1268.1 7.3 bitcast_add_fusion.10
  1275.4 7.7 fusion.240
  1311.4 6.2 fusion.106
  1334.3 7.4 bitcast_convert_fusion
  1341.8 7.0 bitcast_convert_fusion.1
  1357.3 81.9 %all-reduce.8.cloned.1.call-done = bf16[3,1024,512]{2,0,1:T(4,128)(2,1)} async-done(((bf16[3,1024,512]{2,0,1:T(4,128)(2,1)}), bf16[3,1024,512]{2,0,1:T(4,128)(2,1)}) %all-reduce.8.cloned.1.call-update) | async-done | bytes 3145744
  1441.1 58.6 %reduce-scatter.22.cloned.1.call-done = bf16[512,64]{0,1:T(8,128)(2,1)} async-done(((bf16[512,1024]{0,1:T(8,128)(2,1)}), bf16[512,64]{0,1:T(8,128)(2,1)}) %reduce-scatter.22.cloned.1.call-update) | async-done | bytes 65552 | tf_op jit(solution)/shard_map/reduce_scatter | solution.py:267
  1501.2 31.6 %reduce-scatter.20.cloned.1.call-done = bf16[512,1024]{1,0:T(8,128)(2,1)} async-done(((bf16[1024,1024]{1,0:T(8,128)(2,1)}), bf16[512,1024]{1,0:T(8,128)(2,1)}) %reduce-scatter.20.cloned.1.call-update) | async-done | bytes 1048592 | tf_op jit(solution)/shard_map/reduce_scatter | solution.py:249
  1532.8 34.8 %reduce-scatter.16.cloned.1.call-done = bf16[512,1024]{1,0:T(8,128)(2,1)} async-done(((bf16[1024,1024]{1,0:T(8,128)(2,1)}), bf16[512,1024]{1,0:T(8,128)(2,1)}) %reduce-scatter.16.cloned.1.call-update) | async-done | bytes 1048592 | tf_op jit(solution)/shard_map/reduce_scatter | solution.py:249
  1570.9 39.8 %all-reduce.1 = (f32[3,1024]{1,0:T(4,128)}, f32[16]{0:T(128)S(1)}, f32[4096]{0:T(1024)S(1)}) all-reduce(f32[3,1024]{1,0:T(4,128)S(1)} %pad_maximum_fusion.8, f32[16]{0:T(128)S(1)} %add_dynamic-update-slice_fusion.1, f32[4096]{0:T(1024)S(1)} %add_dynamic-update-slice_fusion), channel_id=1, replica_groups=mesh['batch'=16,'tensor'=2] {'batch','tensor'}, use_global_device_ids=true, to_apply=%region_72.73 | all-reduce | flops 7184 | bytes 57472 | tf_op jit(solution)/shard_map/psum | solution.py:286
  (405 shorter events, 250.3 us)
Async XLA Ops:
  7.2 41.6 %all-gather.15.cloned.1.call-start = ((), (), s32[]{:S(2)}) async-start(), calls=%async_computation.9 | async-start | bytes 3145728 | tf_op jit(solution)/shard_map/all_gather | solution.py:156
  12.8 83.4 %all-gather.17.cloned.1.call-start = ((), (), s32[]{:S(2)}) async-start(), calls=%async_computation.10 | async-start | bytes 3342336 | tf_op jit(solution)/shard_map/all_gather | solution.py:125
  13.6 167.3 %all-gather.27.cloned.1.call-start = ((), (), s32[]{:S(2)}) async-start(), calls=%async_computation.16 | async-start | bytes 3145728 | tf_op jit(solution)/shard_map/all_gather | solution.py:156
  14.3 258.1 %all-gather.19.cloned.1.call-start = ((), (), s32[]{:S(2)}) async-start(), calls=%async_computation.11 | async-start | bytes 1114112 | tf_op jit(solution)/shard_map/all_gather | solution.py:126
  14.9 463.9 %all-reduce.10.cloned.1.call-start = ((), (), s32[]{:S(2)}) async-start(), calls=%async_computation.31 | async-start | bytes 16777216 | tf_op jit(solution)/shard_map/psum | solution.py:167
  180.9 7.3 copy-start.46
  266.4 6.0 copy-start.2
  266.4 6.0 copy-start.8
  266.4 6.0 copy-start.48
  281.3 232.4 %all-gather.37.cloned.1.call-start = ((), (), s32[]{:S(2)}) async-start(), calls=%async_computation.29 | async-start | bytes 3145728 | tf_op jit(solution)/shard_map/all_gather | solution.py:193
  284.4 282.0 %all-gather.25.cloned.1.call-start = ((), (), s32[]{:S(2)}) async-start(), calls=%async_computation.14 | async-start | bytes 4456448 | tf_op jit(solution)/shard_map/all_gather | solution.py:128
  285.2 332.5 %all-gather.23.cloned.1.call-start = ((), (), s32[]{:S(2)}) async-start(), calls=%async_computation.13 | async-start | bytes 4456448 | tf_op jit(solution)/shard_map/all_gather | solution.py:127
  285.9 365.5 %all-gather.21.cloned.1.call-start = ((), (), s32[]{:S(2)}) async-start(), calls=%async_computation.12 | async-start | bytes 3145728 | tf_op jit(solution)/shard_map/all_gather | solution.py:175
  490.3 195.7 %all-gather.29.cloned.1.call-start = ((), (), s32[]{:S(2)}) async-start(), calls=%async_computation.17 | async-start | bytes 3145728 | tf_op jit(solution)/shard_map/all_gather | solution.py:175
  490.9 230.2 %all-gather.35.cloned.1.call-start = ((), (), s32[]{:S(2)}) async-start(), calls=%async_computation.28 | async-start | bytes 3145728 | tf_op jit(solution)/shard_map/all_gather | solution.py:193
  491.6 342.9 %reduce-scatter.14.cloned.1.call-start = ((), (), s32[]{:S(2)}) async-start(), calls=%async_computation.19 | async-start | bytes 6291456 | tf_op jit(solution)/shard_map/reduce_scatter | solution.py:215
  661.7 59.4 %copy-start.73 = (f32[2048]{0:T(1024)S(1)}, f32[2048]{0:T(1024)}, u32[]{:S(2)}) copy-start(f32[2048]{0:T(1024)} %param.25) | copy-start | bytes 24580
  748.2 24.7 %copy-start.77 = (bf16[1024,2048]{1,0:T(8,128)(2,1)S(1)}, bf16[1024,2048]{1,0:T(8,128)(2,1)}, u32[]{:S(2)}) copy-start(bf16[1024,2048]{1,0:T(8,128)(2,1)} %all-gather.23.cloned.1.call-done) | copy-start | bytes 12582916
  779.0 90.4 %reduce-scatter.10.cloned.1.call-start = ((), (), s32[]{:S(2)}) async-start(), calls=%async_computation.15 | async-start | bytes 3145728 | tf_op jit(solution)/shard_map/reduce_scatter | solution.py:185
  788.4 137.5 %reduce-scatter.18.cloned.1.call-start = ((), (), s32[]{:S(2)}) async-start(), calls=%async_computation.22 | async-start | bytes 6291456 | tf_op jit(solution)/shard_map/reduce_scatter | solution.py:215
  798.3 161.5 %reduce-scatter.12.cloned.1.call-start = ((), (), s32[]{:S(2)}) async-start(), calls=%async_computation.18 | async-start | bytes 3145728 | tf_op jit(solution)/shard_map/reduce_scatter | solution.py:185
  809.5 192.5 %all-gather.33.cloned.1.call-start = ((), (), s32[]{:S(2)}) async-start(), calls=%async_computation.23 | async-start | bytes 3145728 | tf_op jit(solution)/shard_map/all_gather | solution.py:227
  933.1 32.7 %copy-start.23 = (f32[512,1024]{1,0:T(8,128)S(1)}, f32[512,1024]{1,0:T(8,128)}, u32[]{:S(2)}) copy-start(f32[512,1024]{1,0:T(8,128)} %get-tuple-element.600) | copy-start | bytes 6291460
  959.9 6.3 copy-start.22
  968.5 67.8 %all-gather.31.cloned.1.call-start = ((), (), s32[]{:S(2)}) async-start(), calls=%async_computation.20 | async-start | bytes 3145728 | tf_op jit(solution)/shard_map/all_gather | solution.py:227
  969.1 7.6 copy-start.79
  969.1 381.1 %reduce-scatter.26.cloned.1.call-start = ((), (), s32[]{:S(2)}) async-start(), calls=%async_computation.27 | async-start | bytes 4456448 | tf_op jit(solution)/shard_map/reduce_scatter | solution.py:273
  987.6 364.4 %reduce-scatter.24.cloned.1.call-start = ((), (), s32[]{:S(2)}) async-start(), calls=%async_computation.26 | async-start | bytes 4456448 | tf_op jit(solution)/shard_map/reduce_scatter | solution.py:270
  989.2 6.6 copy-start.33
  989.2 6.6 copy-start.81
  1002.0 437.3 %all-reduce.8.cloned.1.call-start = ((), (), s32[]{:S(2)}) async-start(), calls=%async_computation.30 | async-start | bytes 8388608
  1008.6 32.1 %copy-start.75 = (f32[8]{0:T(128)S(1)}, f32[8]{0:T(128)}, u32[]{:S(2)}) copy-start(f32[8]{0:T(128)} %param.22) | copy-start | bytes 100
  1043.9 124.1 %copy-start.3 = (bf16[1024,8,64]{0,2,1:T(8,128)(2,1)S(1)}, bf16[1024,8,64]{0,2,1:T(8,128)(2,1)}, u32[]{:S(2)}) copy-start(bf16[1024,8,64]{0,2,1:T(8,128)(2,1)} %copy-done.2) | copy-start | bytes 3145732
  1043.9 124.1 %copy-start.37 = (s32[1024]{0:T(1024)S(1)}, s32[1024]{0:T(1024)}, u32[]{:S(2)}) copy-start(s32[1024]{0:T(1024)} %convert_reduce_fusion.2) | copy-start | bytes 12292
  1043.9 124.1 %copy-start.49 = (f32[2,8,512]{2,1,0:T(8,128)S(1)}, f32[2,8,512]{2,1,0:T(8,128)}, u32[]{:S(2)}) copy-start(f32[2,8,512]{2,1,0:T(8,128)} %copy-done.48) | copy-start | bytes 98308
  1086.9 14.3 copy-start
  1147.2 14.9 copy-start
  1209.5 14.4 copy-start.1
  1216.2 7.7 copy-start.16
  1268.1 15.0 copy-start.1
  1275.4 7.7 copy-start.16
  1287.8 7.9 copy-start.7
  1301.2 6.5 copy-start.6
  1311.4 6.3 copy-start.41
  1311.4 6.3 copy-start.44
  1311.4 6.3 copy-start.45
  1311.4 6.3 copy-start.78
  1327.4 172.2 %reduce-scatter.22.cloned.1.call-start = ((), (), s32[]{:S(2)}) async-start(), calls=%async_computation.25 | async-start | bytes 1114112 | tf_op jit(solution)/shard_map/reduce_scatter | solution.py:267
  1334.2 7.6 copy-start.40
  1334.2 7.6 copy-start.43
  1334.2 198.6 %reduce-scatter.20.cloned.1.call-start = ((), (), s32[]{:S(2)}) async-start(), calls=%async_computation.24 | async-start | bytes 3145728 | tf_op jit(solution)/shard_map/reduce_scatter | solution.py:249
  1341.7 7.2 copy-start.82
  1341.7 8.5 copy-start.69
  1341.8 8.5 copy-start.70
  1341.8 225.8 %reduce-scatter.16.cloned.1.call-start = ((), (), s32[]{:S(2)}) async-start(), calls=%async_computation.21 | async-start | bytes 3145728 | tf_op jit(solution)/shard_map/reduce_scatter | solution.py:249
  1348.9 7.9 copy-start.71
  1348.9 8.0 copy-start.72
  1353.8 213.7 %copy-start.12 = (bf16[2,512,1024]{2,1,0:T(8,128)(2,1)S(1)}, bf16[2,512,1024]{2,1,0:T(8,128)(2,1)}, u32[]{:S(2)}) copy-start(bf16[2,512,1024]{2,1,0:T(8,128)(2,1)} %param.18) | copy-start | bytes 6291460
  1353.8 213.7 %copy-start.53 = (f32[1,1024]{1,0:T(1,128)S(1)}, f32[1,1024]{1,0:T(1,128)}, u32[]{:S(2)}) copy-start(f32[1,1024]{1,0:T(1,128)} %copy-done.52) | copy-start | bytes 12292
  1353.8 213.7 %copy-start.55 = (f32[512]{0:T(512)S(1)}, f32[512]{0:T(512)}, u32[]{:S(2)}) copy-start(f32[512]{0:T(512)} %copy-done.54) | copy-start | bytes 6148
  1353.8 213.7 %copy-start.57 = (f32[512]{0:T(512)S(1)}, f32[512]{0:T(512)}, u32[]{:S(2)}) copy-start(f32[512]{0:T(512)} %copy-done.56) | copy-start | bytes 6148
  1353.8 213.7 %copy-start.61 = (f32[512]{0:T(512)S(1)}, f32[512]{0:T(512)}, u32[]{:S(2)}) copy-start(f32[512]{0:T(512)} %copy-done.60) | copy-start | bytes 6148
  1353.9 213.7 %copy-start.63 = (f32[512]{0:T(512)S(1)}, f32[512]{0:T(512)}, u32[]{:S(2)}) copy-start(f32[512]{0:T(512)} %copy-done.62) | copy-start | bytes 6148
  1532.8 79.1 %copy-start.30 = (bf16[512,1024]{1,0:T(8,128)(2,1)S(1)}, bf16[512,1024]{1,0:T(8,128)(2,1)}, u32[]{:S(2)}) copy-start(bf16[512,1024]{1,0:T(8,128)(2,1)} %reduce-scatter.20.cloned.1.call-done) | copy-start | bytes 3145732
  (47 other events, 152.3 us)
Sparse Core Ops, SparseCore 0:
  12.9 35.8 all-gather.14
  51.0 45.2 all-gather.16
  97.8 31.9 all-gather.26
  131.7 37.9 all-gather.18
  281.4 197.3 all-reduce.9
  480.2 33.4 all-gather.36
  515.9 50.5 all-gather.24
  568.6 49.0 all-gather.22
  619.8 31.5 all-gather.20
  652.9 33.1 all-gather.28
  687.6 33.4 all-gather.34
  779.1 55.4 reduce-scatter.13
  837.5 31.8 reduce-scatter.9
  871.5 54.3 reduce-scatter.17
  928.0 31.8 reduce-scatter.11
  968.6 33.1 all-gather.32
  1003.2 33.1 all-gather.30
  1040.1 72.4 reduce-scatter.25
  1116.9 71.3 reduce-scatter.23
  1327.5 111.6 all-reduce.7
  1443.3 56.3 reduce-scatter.21
  1501.9 30.8 reduce-scatter.19
  1535.7 31.8 reduce-scatter.15
where the time goes:
time: 1640 us; the launch traced here: 1620 us
  waiting for transfers between devices  844 us (51%)
  matrix products  385 us (23%)
  other arithmetic  160 us (10%)
  local copies, waits for them, and re-layouts  146 us (9%)
  blocking collectives  53.9 us (3%)
  loops' own time  17.1 us (1%)
    psum x1, waiting for transfers between devices, body(): lax.psum(jnp.dot(scaled, out_full, preferred_element_type=jnp.float32), '...  193 us
    unnamed x24, waiting for transfers between devices  87.2 us
    dynamic_update_slice x8, local copies, waits for them, and re-layouts, attend_forward(): attended, log_sums = lax.map(one_block, firsts)  82.7 us
    reduce_scatter x2, waiting for transfers between devices, body(): lax.psum_scatter(jnp.einsum('gf,df->gd', hidden_grad, up_full, preferred_...  81.5 us
    dot_general x8, matrix products, one_block(): jnp.einsum('qhd,khd->hqk', query_block, all_keys, preferred_element_type=...  73.6 us
    reduce_scatter x2, waiting for transfers between devices, body(): lax.psum_scatter(jnp.einsum('cge,cde->gd', proj_grads, qkv_full, preferre...  66.4 us
    convert_element_type x4, other arithmetic, one_block(): score_grad = (probs * (prob_grad - inner)).astype(jnp.bfloat16)  60 us
    reduce_scatter x2, waiting for transfers between devices, body(): lax.psum_scatter(jnp.dot(narrow, down_full, preferred_element_type=jnp.fl...  58.6 us
  transfers between devices with their start and end apart: 23, of which 18 were waited for; matrix products, arithmetic and copies ran while one was open for 37% of the time, Pallas kernels for 0%

commit v1 on v0

--- a/solution.py
+++ b/solution.py
@@ -164,9 +164,9 @@
             queries, all_keys, values, seg_ids, places, block_rows, factor
         )
         scaled = (attended * head_scale[None, :, None]).astype(jnp.bfloat16).reshape(group_rows, -1)
-        whole_mixed = lax.psum(
-            jnp.dot(scaled, out_full, preferred_element_type=jnp.float32), "tensor"
-        )
+        x = jnp.dot(scaled, out_full, preferred_element_type=jnp.float32)
+        parts = lax.all_gather(x, "tensor")
+        whole_mixed = jnp.sum(parts, axis=0)
         mixed_own = lax.dynamic_slice_in_dim(whole_mixed, row_start, own_rows, 0)
         mixed_unit, mixed_factor = normalize(mixed_own)
         resid = x_rows + mixed_unit * norm_gains[1]

time: 1640 us -> 1550 us (0.945)
  waiting for transfers between devices: 844 us -> 746 us
    psum x1 -> x0, waiting for transfers between devices: 193 us -> none  [body(): lax.psum(jnp.dot(scaled, out_full, preferred_element_type=jnp.float32), '...]
    all_gather x0 -> x2, waiting for transfers between devices: none -> 103 us  [body(): parts = lax.all_gather(x, 'tensor')]
    unnamed x24 -> x25, waiting for transfers between devices: 87.2 us -> 86.9 us
  transfers between devices with their start and end apart: 23 -> 24, of which waited for: 18 -> 19; matrix products, arithmetic and copies ran while one was open for 37% -> 40% of each run, Pallas kernels for 0% -> 0%
where the time goes in v1:
time: 1550 us; the launch traced here: 1540 us
  waiting for transfers between devices  746 us (48%)
  matrix products  385 us (25%)
  other arithmetic  174 us (11%)
  local copies, waits for them, and re-layouts  149 us (10%)
  blocking collectives  53.9 us (3%)
  loops' own time  16.8 us (1%)
  between operations  16.6 us (1%)
    all_gather x2, waiting for transfers between devices, body(): parts = lax.all_gather(x, 'tensor')  103 us
    unnamed x25, waiting for transfers between devices  86.9 us
    dynamic_update_slice x8, local copies, waits for them, and re-layouts, attend_forward(): attended, log_sums = lax.map(one_block, firsts)  82.7 us
    reduce_scatter x2, waiting for transfers between devices, body(): lax.psum_scatter(jnp.einsum('gf,df->gd', hidden_grad, up_full, preferred_...  81.5 us
    dot_general x8, matrix products, one_block(): jnp.einsum('qhd,khd->hqk', query_block, all_keys, preferred_element_type=...  73.7 us
    reduce_scatter x2, waiting for transfers between devices, body(): lax.psum_scatter(jnp.einsum('cge,cde->gd', proj_grads, qkv_full, preferre...  65.7 us
    convert_element_type x4, other arithmetic, one_block(): score_grad = (probs * (prob_grad - inner)).astype(jnp.bfloat16)  60.1 us
    reduce_scatter x2, waiting for transfers between devices, body(): lax.psum_scatter(jnp.dot(narrow, down_full, preferred_element_type=jnp.fl...  58.6 us
  transfers between devices with their start and end apart: 24, of which 19 were waited for; matrix products, arithmetic and copies ran while one was open for 40% of the time, Pallas kernels for 0%

profile of v1, /device:TPU:0, one launch (start us, length us, event | category | flops | bytes accessed | tf_op | source)
XLA Modules:
  0.0 1542.2 jit_solution(8849034299626364733)
XLA Ops:
  16.8 32.0 %all-gather.19.cloned.1.call-done = bf16[1024,1024]{1,0:T(8,128)(2,1)} async-done(((bf16[512,1024]{1,0:T(8,128)(2,1)}), bf16[1024,1024]{1,0:T(8,128)(2,1)}) %all-gather.19.cloned.1.call-update) | async-done | bytes 2097168 | tf_op jit(solution)/shard_map/all_gather | solution.py:156
  48.8 47.4 %all-gather.21.cloned.1.call-done = bf16[3,1024,512]{2,1,0:T(8,128)(2,1)} async-done(((bf16[3,64,512]{2,1,0:T(8,128)(2,1)}), bf16[3,1024,512]{2,1,0:T(8,128)(2,1)}) %all-gather.21.cloned.1.call-update) | async-done | bytes 3145744 | tf_op jit(solution)/shard_map/all_gather | solution.py:125
  105.5 75.0 %while.58 = (s32[]{:T(128)}, f32[2,512,8,64]{1,0,3,2:T(2,128)}, f32[2,8,512]{2,1,0:T(8,128)S(1)}, s32[2]{0:T(128)S(1)}, s32[1024]{0:T(1024)S(1)}, /*index=5*/s32...) while((s32[]{:T(128)}, f32[2,512,8,64]{1,0,3,2:T(2,128)}, ...), condition=%wide.region_7.8_spmd.clone, body=%wide.region_4.7_spmd.clone.sunk | while | flops 1125642240 | bytes 60444856 | solution.py:57
  123.5 19.6 %dynamic_update_slice.49 = f32[2,512,8,64]{1,0,3,2:T(2,128)} dynamic-update-slice(f32[2,512,8,64]{1,0,3,2:T(2,128)} %get-tuple-element.982, f32[1,512,8,64]{1,0,3,2:T(1,128)S(1)} %copy.131, s32[]{:T(128)} %get-tuple-element.981, s32[]{:T(128)} %constant.141.clone.1..sunk, s32[]{:T(128)} %constant.141.clone.1..sunk, s32[]{:T(128)} %constant.141.clone.1..sunk) | dynamic-update-slice | bytes 2097156 | tf_op jit(solution)/shard_map/while/body/jit(dynamic_update_index_in_dim)/dynamic_update_slice | solution.py:57
  160.9 19.6 %dynamic_update_slice.49 = f32[2,512,8,64]{1,0,3,2:T(2,128)} dynamic-update-slice(f32[2,512,8,64]{1,0,3,2:T(2,128)} %get-tuple-element.982, f32[1,512,8,64]{1,0,3,2:T(1,128)S(1)} %copy.131, s32[]{:T(128)} %get-tuple-element.981, s32[]{:T(128)} %constant.141.clone.1..sunk, s32[]{:T(128)} %constant.141.clone.1..sunk, s32[]{:T(128)} %constant.141.clone.1..sunk) | dynamic-update-slice | bytes 2097156 | tf_op jit(solution)/shard_map/while/body/jit(dynamic_update_index_in_dim)/dynamic_update_slice | solution.py:57
  200.8 75.0 %while.59 = (s32[]{:T(128)}, f32[2,512,8,64]{1,0,3,2:T(2,128)}, f32[2,8,512]{2,1,0:T(8,128)S(1)}, s32[2]{0:T(128)S(1)}, s32[1024]{0:T(1024)S(1)}, /*index=5*/s32...) while((s32[]{:T(128)}, f32[2,512,8,64]{1,0,3,2:T(2,128)}, ...), condition=%wide.region_25.26_spmd.clone, body=%wide.region_22.25_spmd.clone.sunk | while | flops 1125642240 | bytes 60444856 | solution.py:57
  218.7 19.6 %dynamic_update_slice.51 = f32[2,512,8,64]{1,0,3,2:T(2,128)} dynamic-update-slice(f32[2,512,8,64]{1,0,3,2:T(2,128)} %get-tuple-element.946, f32[1,512,8,64]{1,0,3,2:T(1,128)S(1)} %copy.132, s32[]{:T(128)} %get-tuple-element.945, s32[]{:T(128)} %constant.141.clone.1..sunk.1, s32[]{:T(128)} %constant.141.clone.1..sunk.1, s32[]{:T(128)} %constant.141.clone.1..sunk.1) | dynamic-update-slice | bytes 2097156 | tf_op jit(solution)/shard_map/while/body/jit(dynamic_update_index_in_dim)/dynamic_update_slice | solution.py:57
  256.1 19.6 %dynamic_update_slice.51 = f32[2,512,8,64]{1,0,3,2:T(2,128)} dynamic-update-slice(f32[2,512,8,64]{1,0,3,2:T(2,128)} %get-tuple-element.946, f32[1,512,8,64]{1,0,3,2:T(1,128)S(1)} %copy.132, s32[]{:T(128)} %get-tuple-element.945, s32[]{:T(128)} %constant.141.clone.1..sunk.1, s32[]{:T(128)} %constant.141.clone.1..sunk.1, s32[]{:T(128)} %constant.141.clone.1..sunk.1) | dynamic-update-slice | bytes 2097156 | tf_op jit(solution)/shard_map/while/body/jit(dynamic_update_index_in_dim)/dynamic_update_slice | solution.py:57
  292.9 6.7 reduce_sum.467
  299.6 98.8 %all-gather.41.cloned.1.call-done = f32[2048,1024]{1,0:T(8,128)} async-done(((f32[1024,1024]{1,0:T(8,128)}), f32[2048,1024]{1,0:T(8,128)}) %all-gather.41.cloned.1.call-update) | async-done | bytes 8388624 | tf_op jit(solution)/shard_map/all_gather | solution.py:168
  398.4 6.6 reduce_sum.477
  418.4 14.6 all-gather.45.cloned.1.call-done
  433.1 52.8 %all-gather.29.cloned.1.call-done = bf16[2048,1024]{0,1:T(8,128)(2,1)} async-done(((bf16[2048,64]{0,1:T(8,128)(2,1)}), bf16[2048,1024]{0,1:T(8,128)(2,1)}) %all-gather.29.cloned.1.call-update) | async-done | bytes 4194320 | tf_op jit(solution)/shard_map/all_gather | solution.py:128
  485.8 10.5 fusion.98
  496.4 40.9 %all-gather.27.cloned.1.call-done = bf16[1024,2048]{1,0:T(8,128)(2,1)} async-done(((bf16[64,2048]{1,0:T(8,128)(2,1)}), bf16[1024,2048]{1,0:T(8,128)(2,1)}) %all-gather.27.cloned.1.call-update) | async-done | bytes 4194320 | tf_op jit(solution)/shard_map/all_gather | solution.py:127
  537.3 33.6 %all-gather.25.cloned.1.call-done = bf16[1024,1024]{1,0:T(8,128)(2,1)} async-done(((bf16[512,1024]{1,0:T(8,128)(2,1)}), bf16[1024,1024]{1,0:T(8,128)(2,1)}) %all-gather.25.cloned.1.call-update) | async-done | bytes 2097168 | tf_op jit(solution)/shard_map/all_gather | solution.py:175
  570.9 10.2 fusion.120
  581.1 24.5 %all-gather.33.cloned.1.call-done = bf16[1024,1024]{1,0:T(8,128)(2,1)} async-done(((bf16[512,1024]{1,0:T(8,128)(2,1)}), bf16[1024,1024]{1,0:T(8,128)(2,1)}) %all-gather.33.cloned.1.call-update) | async-done | bytes 2097168 | tf_op jit(solution)/shard_map/all_gather | solution.py:175
  605.6 10.0 fusion.121
  615.6 7.2 all-reduce.3
  622.8 17.7 %all-gather.43.cloned.1.call-done = bf16[1,1024,1024]{2,1,0:T(8,128)(2,1)} async-done(((bf16[1,512,1024]{2,1,0:T(8,128)(2,1)}), bf16[1,1024,1024]{2,1,0:T(8,128)(2,1)}) %all-gather.43.cloned.1.call-update) | async-done | bytes 2097168 | tf_op jit(solution)/shard_map/all_gather | solution.py:193
  640.5 20.2 %multiply_reduce_fusion.3 = (f32[2048]{0:T(1024)}, f32[1024]{0:T(1024)S(1)}, f32[1024]{0:T(1024)S(1)}, f32[1024]{0:T(1024)S(1)}, f32[1024]{0:T(1024)S(1)}, /*index=5*/f32[2048]{0:T(1024)}, f32[1024,2048]{1,0:T(8,128)}) fusion(f32[1024]{0:T(1024)S(1)} %get-tuple-element.643, f32[1024]{0:T(1024)S(1)} %get-tuple-element.642, ...), kind=kOutput, calls=%fused_computation.90 | convolution fusion | flops 4362067968 | bytes 39903232 | tf_op jit(solution)/shard_map/gd,fd->gf/dot_general | solution.py:197
  660.6 6.9 all-reduce.2
  667.6 22.7 %fusion.54 = (bf16[1024,2048]{1,0:T(8,128)(2,1)S(1)}, bf16[1024,2048]{1,0:T(8,128)(2,1)}, bf16[1024,2048]{1,0:T(8,128)(2,1)}) fusion(f32[1024,2048]{1,0:T(8,128)} %get-tuple-element.653, f32[1024,2048]{1,0:T(8,128)} %get-tuple-element.654, f32[1024]{0:T(1024)S(1)} %get-tuple-element.592, f32[1024]{0:T(1024)S(1)} %broadcast_multiply_fusion.1, ...), kind=kLoop, calls=%fused_computation.80 | loop fusion | flops 125829120 | bytes 46178304 | tf_op jit(solution)/shard_map/convert_element_type | solution.py:211
  698.4 9.3 convolution_convert_fusion.1
  707.8 9.9 fusion.131
  717.8 11.1 convolution_convert_fusion
  729.0 25.0 %reduce-scatter.14.cloned.1.call-done = f32[512,1024]{1,0:T(8,128)} async-done(((f32[1024,1024]{1,0:T(8,128)}), f32[512,1024]{1,0:T(8,128)}) %reduce-scatter.14.cloned.1.call-update) | async-done | bytes 2097168 | tf_op jit(solution)/shard_map/reduce_scatter | solution.py:215
  757.0 31.6 %reduce-scatter.10.cloned.1.call-done = bf16[512,1024]{1,0:T(8,128)(2,1)} async-done(((bf16[1024,1024]{1,0:T(8,128)(2,1)}), bf16[512,1024]{1,0:T(8,128)(2,1)}) %reduce-scatter.10.cloned.1.call-update) | async-done | bytes 1048592 | tf_op jit(solution)/shard_map/reduce_scatter | solution.py:185
  788.6 56.5 %reduce-scatter.18.cloned.1.call-done = f32[512,1024]{1,0:T(8,128)} async-done(((f32[1024,1024]{1,0:T(8,128)}), f32[512,1024]{1,0:T(8,128)}) %reduce-scatter.18.cloned.1.call-update) | async-done | bytes 2097168 | tf_op jit(solution)/shard_map/reduce_scatter | solution.py:215
  845.1 7.1 multiply_reduce_fusion.15
  852.2 26.9 %reduce-scatter.12.cloned.1.call-done = bf16[512,1024]{1,0:T(8,128)(2,1)} async-done(((bf16[1024,1024]{1,0:T(8,128)(2,1)}), bf16[512,1024]{1,0:T(8,128)(2,1)}) %reduce-scatter.12.cloned.1.call-update) | async-done | bytes 1048592 | tf_op jit(solution)/shard_map/reduce_scatter | solution.py:185
  888.4 7.6 fusion.100
  896.0 10.9 add_convert_fusion
  927.9 27.7 %all-gather.35.cloned.1.call-done = bf16[1024,1024]{1,0:T(8,128)(2,1)} async-done(((bf16[512,1024]{1,0:T(8,128)(2,1)}), bf16[1024,1024]{1,0:T(8,128)(2,1)}) %all-gather.35.cloned.1.call-update) | async-done | bytes 2097168 | tf_op jit(solution)/shard_map/all_gather | solution.py:227
  962.6 123.2 %while.60 = (s32[]{:T(128)}, f32[1024,8,64]{0,2,1:T(8,128)}, f32[1024,8,64]{0,2,1:T(8,128)}, bf16[2,512,8,64]{1,3,2,0:T(8,128)(2,1)}, s32[2]{0:T(128)S(1)}, /*in...) while((s32[]{:T(128)}, f32[1024,8,64]{0,2,1:T(8,128)}, ...), condition=%wide.region_47.48_spmd.clone.clone, body=%wide.region_45.47_spmd.clone.clone.sunk | while | flops 2726555648 | bytes 208769808 | solution.py:104
  966.2 10.5 fusion.228
  976.7 14.0 multiply_reduce_fusion.30
  990.7 14.9 multiply_convert_fusion.20
  1005.6 6.8 bitcast_add_fusion.8
  1012.3 7.7 fusion.229
  1027.3 9.6 fusion.228
  1036.9 13.6 multiply_reduce_fusion.30
  1050.5 15.5 %multiply_convert_fusion.20 = bf16[8,512,1024]{2,1,0:T(8,128)(2,1)} fusion(f32[8,512,1024]{2,1,0:T(8,128)} %get-tuple-element.917, f32[8,512,1024]{2,1,0:T(8,128)} %fusion.228, f32[8,512]{1,0:T(8,128)S(1)} %get-tuple-element.918), kind=kLoop, calls=%fused_computation.28.clone.1 | loop fusion | flops 12582912 | bytes 41959424 | tf_op jit(solution)/shard_map/while/body/eval_jaxpr/convert_element_type | solution.py:88
  1066.0 7.3 bitcast_add_fusion.8
  1073.3 7.6 fusion.229
  1086.8 119.6 %while.61 = (s32[]{:T(128)}, f32[1024,8,64]{0,2,1:T(8,128)}, f32[1024,8,64]{0,2,1:T(8,128)}, bf16[2,512,8,64]{1,3,2,0:T(8,128)(2,1)}, s32[2]{0:T(128)S(1)}, /*in...) while((s32[]{:T(128)}, f32[1024,8,64]{0,2,1:T(8,128)}, ...), condition=%wide.region_62.63_spmd.clone.clone, body=%wide.region_60.62_spmd.clone.clone.sunk | while | flops 2726555648 | bytes 212964144 | solution.py:104
  1090.2 9.6 fusion.239
  1099.8 13.7 multiply_reduce_fusion.31
  1113.5 14.8 multiply_convert_fusion.21
  1128.3 6.7 bitcast_add_fusion.10
  1135.0 7.7 fusion.240
  1148.9 9.6 fusion.239
  1158.5 13.6 multiply_reduce_fusion.31
  1172.1 14.8 multiply_convert_fusion.21
  1186.9 7.2 bitcast_add_fusion.10
  1194.1 7.7 fusion.240
  1253.4 7.5 bitcast_convert_fusion
  1261.0 7.0 bitcast_convert_fusion.1
  1276.5 81.6 %all-reduce.6.cloned.1.call-done = bf16[3,1024,512]{2,0,1:T(4,128)(2,1)} async-done(((bf16[3,1024,512]{2,0,1:T(4,128)(2,1)}), bf16[3,1024,512]{2,0,1:T(4,128)(2,1)}) %all-reduce.6.cloned.1.call-update) | async-done | bytes 3145744
  1359.9 58.6 %reduce-scatter.22.cloned.1.call-done = bf16[512,64]{0,1:T(8,128)(2,1)} async-done(((bf16[512,1024]{0,1:T(8,128)(2,1)}), bf16[512,64]{0,1:T(8,128)(2,1)}) %reduce-scatter.22.cloned.1.call-update) | async-done | bytes 65552 | tf_op jit(solution)/shard_map/reduce_scatter | solution.py:267
  1420.0 31.6 %reduce-scatter.20.cloned.1.call-done = bf16[512,1024]{1,0:T(8,128)(2,1)} async-done(((bf16[1024,1024]{1,0:T(8,128)(2,1)}), bf16[512,1024]{1,0:T(8,128)(2,1)}) %reduce-scatter.20.cloned.1.call-update) | async-done | bytes 1048592 | tf_op jit(solution)/shard_map/reduce_scatter | solution.py:249
  1451.6 34.0 %reduce-scatter.16.cloned.1.call-done = bf16[512,1024]{1,0:T(8,128)(2,1)} async-done(((bf16[1024,1024]{1,0:T(8,128)(2,1)}), bf16[512,1024]{1,0:T(8,128)(2,1)}) %reduce-scatter.16.cloned.1.call-update) | async-done | bytes 1048592 | tf_op jit(solution)/shard_map/reduce_scatter | solution.py:249
  1489.0 39.8 %all-reduce.1 = (f32[3,1024]{1,0:T(4,128)}, f32[16]{0:T(128)S(1)}, f32[4096]{0:T(1024)S(1)}) all-reduce(f32[3,1024]{1,0:T(4,128)S(1)} %pad_maximum_fusion.8, f32[16]{0:T(128)S(1)} %add_dynamic-update-slice_fusion.1, f32[4096]{0:T(1024)S(1)} %add_dynamic-update-slice_fusion), channel_id=1, replica_groups=mesh['batch'=16,'tensor'=2] {'batch','tensor'}, use_global_device_ids=true, to_apply=%region_72.73 | all-reduce | flops 7184 | bytes 57472 | tf_op jit(solution)/shard_map/psum | solution.py:286
  (414 shorter events, 270.7 us)
Async XLA Ops:
  7.2 41.6 %all-gather.19.cloned.1.call-start = ((), (), s32[]{:S(2)}) async-start(), calls=%async_computation.9 | async-start | bytes 3145728 | tf_op jit(solution)/shard_map/all_gather | solution.py:156
  12.8 83.4 %all-gather.21.cloned.1.call-start = ((), (), s32[]{:S(2)}) async-start(), calls=%async_computation.10 | async-start | bytes 3342336 | tf_op jit(solution)/shard_map/all_gather | solution.py:125
  13.6 171.1 %all-gather.23.cloned.1.call-start = ((), (), s32[]{:S(2)}) async-start(), calls=%async_computation.11 | async-start | bytes 1114112 | tf_op jit(solution)/shard_map/all_gather | solution.py:126
  14.3 175.7 %all-gather.31.cloned.1.call-start = ((), (), s32[]{:S(2)}) async-start(), calls=%async_computation.16 | async-start | bytes 3145728 | tf_op jit(solution)/shard_map/all_gather | solution.py:156
  14.9 278.1 %all-gather.39.cloned.1.call-start = ((), (), s32[]{:S(2)}) async-start(), calls=%async_computation.28 | async-start | bytes 12582912 | tf_op jit(solution)/shard_map/all_gather | solution.py:168
  180.5 9.4 copy-start.2
  180.5 9.4 copy-start.8
  180.5 9.4 copy-start.38
  180.5 9.4 copy-start.46
  189.9 208.4 %all-gather.41.cloned.1.call-start = ((), (), s32[]{:S(2)}) async-start(), calls=%async_computation.29 | async-start | bytes 12582912 | tf_op jit(solution)/shard_map/all_gather | solution.py:168
  275.8 7.6 copy-start.4
  275.9 7.6 copy-start.9
  275.9 7.6 copy-start.48
  275.9 7.6 copy-start.85
  283.5 149.6 %all-gather.45.cloned.1.call-start = ((), (), s32[]{:S(2)}) async-start(), calls=%async_computation.31 | async-start | bytes 3145728 | tf_op jit(solution)/shard_map/all_gather | solution.py:193
  286.7 199.1 %all-gather.29.cloned.1.call-start = ((), (), s32[]{:S(2)}) async-start(), calls=%async_computation.14 | async-start | bytes 4456448 | tf_op jit(solution)/shard_map/all_gather | solution.py:128
  287.5 249.8 %all-gather.27.cloned.1.call-start = ((), (), s32[]{:S(2)}) async-start(), calls=%async_computation.13 | async-start | bytes 4456448 | tf_op jit(solution)/shard_map/all_gather | solution.py:127
  288.2 282.6 %all-gather.25.cloned.1.call-start = ((), (), s32[]{:S(2)}) async-start(), calls=%async_computation.12 | async-start | bytes 3145728 | tf_op jit(solution)/shard_map/all_gather | solution.py:175
  417.1 188.5 %all-gather.33.cloned.1.call-start = ((), (), s32[]{:S(2)}) async-start(), calls=%async_computation.17 | async-start | bytes 3145728 | tf_op jit(solution)/shard_map/all_gather | solution.py:175
  417.8 222.7 %all-gather.43.cloned.1.call-start = ((), (), s32[]{:S(2)}) async-start(), calls=%async_computation.30 | async-start | bytes 3145728 | tf_op jit(solution)/shard_map/all_gather | solution.py:193
  418.4 335.6 %reduce-scatter.14.cloned.1.call-start = ((), (), s32[]{:S(2)}) async-start(), calls=%async_computation.19 | async-start | bytes 6291456 | tf_op jit(solution)/shard_map/reduce_scatter | solution.py:215
  581.1 59.4 %copy-start.74 = (f32[2048]{0:T(1024)S(1)}, f32[2048]{0:T(1024)}, u32[]{:S(2)}) copy-start(f32[2048]{0:T(1024)} %param.25) | copy-start | bytes 24580
  667.6 24.7 %copy-start.78 = (bf16[1024,2048]{1,0:T(8,128)(2,1)S(1)}, bf16[1024,2048]{1,0:T(8,128)(2,1)}, u32[]{:S(2)}) copy-start(bf16[1024,2048]{1,0:T(8,128)(2,1)} %all-gather.27.cloned.1.call-done) | copy-start | bytes 12582916
  698.4 90.2 %reduce-scatter.10.cloned.1.call-start = ((), (), s32[]{:S(2)}) async-start(), calls=%async_computation.15 | async-start | bytes 3145728 | tf_op jit(solution)/shard_map/reduce_scatter | solution.py:185
  707.8 137.3 %reduce-scatter.18.cloned.1.call-start = ((), (), s32[]{:S(2)}) async-start(), calls=%async_computation.22 | async-start | bytes 6291456 | tf_op jit(solution)/shard_map/reduce_scatter | solution.py:215
  717.8 161.4 %reduce-scatter.12.cloned.1.call-start = ((), (), s32[]{:S(2)}) async-start(), calls=%async_computation.18 | async-start | bytes 3145728 | tf_op jit(solution)/shard_map/reduce_scatter | solution.py:185
  729.0 192.3 %all-gather.37.cloned.1.call-start = ((), (), s32[]{:S(2)}) async-start(), calls=%async_computation.23 | async-start | bytes 3145728 | tf_op jit(solution)/shard_map/all_gather | solution.py:227
  852.2 32.9 %copy-start.24 = (f32[512,1024]{1,0:T(8,128)S(1)}, f32[512,1024]{1,0:T(8,128)}, u32[]{:S(2)}) copy-start(f32[512,1024]{1,0:T(8,128)} %get-tuple-element.598) | copy-start | bytes 6291460
  887.7 67.8 %all-gather.35.cloned.1.call-start = ((), (), s32[]{:S(2)}) async-start(), calls=%async_computation.20 | async-start | bytes 3145728 | tf_op jit(solution)/shard_map/all_gather | solution.py:227
  888.3 7.6 copy-start.81
  888.3 381.1 %reduce-scatter.26.cloned.1.call-start = ((), (), s32[]{:S(2)}) async-start(), calls=%async_computation.27 | async-start | bytes 4456448 | tf_op jit(solution)/shard_map/reduce_scatter | solution.py:273
  906.9 364.4 %reduce-scatter.24.cloned.1.call-start = ((), (), s32[]{:S(2)}) async-start(), calls=%async_computation.26 | async-start | bytes 4456448 | tf_op jit(solution)/shard_map/reduce_scatter | solution.py:270
  908.4 6.6 copy-start.83
  921.2 34.4 %copy-start.20 = (f32[64,8,2,512]{3,1,2,0:T(8,128)S(1)}, f32[64,8,2,512]{3,1,2,0:T(8,128)}, u32[]{:S(2)}) copy-start(f32[64,8,2,512]{3,1,2,0:T(8,128)} %copy.127) | copy-start | bytes 6291460
  921.2 436.9 %all-reduce.6.cloned.1.call-start = ((), (), s32[]{:S(2)}) async-start(), calls=%async_computation.32 | async-start | bytes 8388608
  927.9 31.4 %copy-start.76 = (f32[8]{0:T(128)S(1)}, f32[8]{0:T(128)}, u32[]{:S(2)}) copy-start(f32[8]{0:T(128)} %param.22) | copy-start | bytes 100
  962.5 124.3 %copy-start.5 = (bf16[1024,8,64]{0,2,1:T(8,128)(2,1)S(1)}, bf16[1024,8,64]{0,2,1:T(8,128)(2,1)}, u32[]{:S(2)}) copy-start(bf16[1024,8,64]{0,2,1:T(8,128)(2,1)} %copy-done.4) | copy-start | bytes 3145732
  962.5 124.3 %copy-start.37 = (s32[1024]{0:T(1024)S(1)}, s32[1024]{0:T(1024)}, u32[]{:S(2)}) copy-start(s32[1024]{0:T(1024)} %convert_reduce_fusion.2) | copy-start | bytes 12292
  962.5 124.3 %copy-start.49 = (f32[2,8,512]{2,1,0:T(8,128)S(1)}, f32[2,8,512]{2,1,0:T(8,128)}, u32[]{:S(2)}) copy-start(f32[2,8,512]{2,1,0:T(8,128)} %copy-done.48) | copy-start | bytes 98308
  1005.6 14.4 copy-start
  1066.0 14.9 copy-start
  1128.3 14.3 copy-start.1
  1135.0 7.7 copy-start.19
  1186.9 14.9 copy-start.1
  1194.1 7.7 copy-start.19
  1206.5 7.9 copy-start.7
  1219.9 6.6 copy-start.6
  1246.2 172.2 %reduce-scatter.22.cloned.1.call-start = ((), (), s32[]{:S(2)}) async-start(), calls=%async_computation.25 | async-start | bytes 1114112 | tf_op jit(solution)/shard_map/reduce_scatter | solution.py:267
  1253.3 7.7 copy-start.40
  1253.4 7.7 copy-start.43
  1253.4 198.3 %reduce-scatter.20.cloned.1.call-start = ((), (), s32[]{:S(2)}) async-start(), calls=%async_computation.24 | async-start | bytes 3145728 | tf_op jit(solution)/shard_map/reduce_scatter | solution.py:249
  1260.9 7.2 copy-start.84
  1260.9 8.4 copy-start.70
  1260.9 8.4 copy-start.71
  1261.0 224.7 %reduce-scatter.16.cloned.1.call-start = ((), (), s32[]{:S(2)}) async-start(), calls=%async_computation.21 | async-start | bytes 3145728 | tf_op jit(solution)/shard_map/reduce_scatter | solution.py:249
  1268.1 7.9 copy-start.72
  1268.1 8.0 copy-start.73
  1273.0 212.7 %copy-start.12 = (bf16[2,512,1024]{2,1,0:T(8,128)(2,1)S(1)}, bf16[2,512,1024]{2,1,0:T(8,128)(2,1)}, u32[]{:S(2)}) copy-start(bf16[2,512,1024]{2,1,0:T(8,128)(2,1)} %param.18) | copy-start | bytes 6291460
  1273.0 212.7 %copy-start.53 = (f32[1,1024]{1,0:T(1,128)S(1)}, f32[1,1024]{1,0:T(1,128)}, u32[]{:S(2)}) copy-start(f32[1,1024]{1,0:T(1,128)} %copy-done.52) | copy-start | bytes 12292
  1273.0 212.7 %copy-start.55 = (f32[512]{0:T(512)S(1)}, f32[512]{0:T(512)}, u32[]{:S(2)}) copy-start(f32[512]{0:T(512)} %copy-done.54) | copy-start | bytes 6148
  1273.0 212.7 %copy-start.57 = (f32[512]{0:T(512)S(1)}, f32[512]{0:T(512)}, u32[]{:S(2)}) copy-start(f32[512]{0:T(512)} %copy-done.56) | copy-start | bytes 6148
  1273.0 212.7 %copy-start.62 = (f32[512]{0:T(512)S(1)}, f32[512]{0:T(512)}, u32[]{:S(2)}) copy-start(f32[512]{0:T(512)} %copy-done.61) | copy-start | bytes 6148
  1273.0 212.7 %copy-start.64 = (f32[512]{0:T(512)S(1)}, f32[512]{0:T(512)}, u32[]{:S(2)}) copy-start(f32[512]{0:T(512)} %copy-done.63) | copy-start | bytes 6148
  1451.6 78.4 %copy-start.30 = (bf16[512,1024]{1,0:T(8,128)(2,1)S(1)}, bf16[512,1024]{1,0:T(8,128)(2,1)}, u32[]{:S(2)}) copy-start(bf16[512,1024]{1,0:T(8,128)(2,1)} %reduce-scatter.20.cloned.1.call-done) | copy-start | bytes 3145732
  (50 other events, 178.8 us)
Sparse Core Ops, SparseCore 0:
  12.9 35.8 all-gather.18
  51.0 45.2 all-gather.20
  98.4 36.8 all-gather.22
  136.6 32.0 all-gather.30
  190.1 102.8 all-gather.38
  294.3 103.9 all-gather.40
  399.9 33.1 all-gather.44
  435.2 50.5 all-gather.28
  488.0 49.2 all-gather.26
  539.2 31.5 all-gather.24
  572.4 33.1 all-gather.32
  607.0 33.4 all-gather.42
  698.5 55.4 reduce-scatter.13
  756.7 31.8 reduce-scatter.9
  790.7 54.3 reduce-scatter.17
  847.3 31.8 reduce-scatter.11
  887.9 33.1 all-gather.36
  922.4 33.1 all-gather.34
  959.4 72.4 reduce-scatter.25
  1036.1 71.3 reduce-scatter.23
  1246.4 111.6 all-reduce.5
  1362.1 56.3 reduce-scatter.21
  1420.7 30.8 reduce-scatter.19
  1453.8 31.8 reduce-scatter.15
